TPU v7x, 256 devices: a whole 4x4x8 slice. The times are simulated.
256 devices in a mesh: section: 4 (over y), ctx: 64 (over z, x, core).
Axes of the slice: x: 4, y: 4, z: 8, core: 2. Of those that a mesh axis runs over, the one named last changes fastest.
Arguments:
- incoming: bfloat16 [4, 8192, 4096], P('section', 'ctx'), may hold values from -6 to 6
- layer_input: bfloat16 [4, 8192, 4096], P('section', 'ctx'), may hold values from -6 to 6
- pre_gate: bfloat16 [4, 8192, 4096], P('section', 'ctx'), may hold values from -6 to 6
- mid_gate: bfloat16 [4, 8192, 4096], P('section', 'ctx'), may hold values from -6 to 6
- long_gate: bfloat16 [4, 8192, 4096], P('section', 'ctx'), may hold values from -6 to 6
- out_gate: bfloat16 [4, 8192, 4096], P('section', 'ctx'), may hold values from -6 to 6
- long_filter: bfloat16 [4, 4096, 8192], P('section', 'ctx'), may hold values from -0.0625 to 0.0625
- mid_filter: bfloat16 [4, 128, 4096], P('section'), may hold values from -0.5 to 0.5
Outputs:
- input_grad: bfloat16 [4, 8192, 4096], P('section', 'ctx')
- long_grad: bfloat16 [4, 4096, 8192], P('section', 'ctx')
- mid_grad: bfloat16 [4, 128, 4096], P('section', None, 'ctx')
All inputs are finite; a program needn't handle non-finite values.
Results may differ from a plain program's by a relative error of at most 0.008.
Values may be sent and summed in bfloat16 or wider, within the bound.
A program may use at most 192 MiB of HBM per device.

v0:
```python
import math
import jax
import jax.numpy as jnp
from jax import lax
from jax.sharding import PartitionSpec as P


def passed_along(value, axis, steps):
    count = lax.axis_size(axis)
    pairs = [(source, (source + steps) % count) for source in range(count)]
    return lax.ppermute(value, axis, pairs)


def shifted(array, axis, by):
    devices = lax.axis_size(axis)
    pairs = [(i, i + by) for i in range(devices) if 0 <= i + by < devices]
    return lax.ppermute(array, axis, pairs)


def unit_roots(rows, cols, period):
    row_ids = jnp.arange(rows, dtype=jnp.int32)[:, None]
    col_ids = jnp.arange(cols, dtype=jnp.int32)[None, :]
    angle = (row_ids * col_ids % period).astype(jnp.float32) * (-2.0 * math.pi / period)
    return (jnp.cos(angle), jnp.sin(angle))


def contract(form, left, right):
    return jnp.einsum(
        form, left, right, precision=lax.Precision.HIGH, preferred_element_type=jnp.float32
    )


def to_spectrum(parts, factor_a, factor_b):
    channels = parts.shape[0]
    inputs_count = parts.shape[1]
    half = factor_a // 2
    period = factor_a * factor_b
    fa_cos, fa_sin = unit_roots(factor_a, half, factor_a)
    first_table = jnp.stack([jnp.stack([fa_cos, -fa_sin]), jnp.stack([fa_sin, fa_cos])])[
        :, :inputs_count
    ]
    tw_cos, tw_sin = unit_roots(factor_a, factor_b, period)
    fb_cos, fb_sin = unit_roots(factor_b, factor_b, factor_b)
    second_table = jnp.stack([jnp.stack([fb_cos, fb_sin]), jnp.stack([-fb_sin, fb_cos])])
    shaped = parts.reshape(channels, inputs_count, half, factor_b)
    first = contract("qrca,nrab->nqcb", first_table, shaped)
    first_re = first[:, 0]
    first_im = first[:, 1]
    turned = jnp.stack(
        [first_re * tw_cos - first_im * tw_sin, first_re * tw_sin + first_im * tw_cos], 1
    )
    return contract("nqcb,qpbd->npcd", turned, second_table)


def from_spectrum(spectrum, factor_a, factor_b, scale):
    channels = spectrum.shape[0]
    half = factor_a // 2
    period = factor_a * factor_b
    fb_cos, fb_sin = unit_roots(factor_b, factor_b, factor_b)
    back_table = jnp.stack([jnp.stack([fb_cos, -fb_sin]), jnp.stack([fb_sin, fb_cos])])
    tw_cos, tw_sin = unit_roots(factor_a, factor_b, period)
    fa_cos, fa_sin = unit_roots(half, factor_a, factor_a)
    last_table = jnp.stack(
        [
            jnp.stack([fa_cos, fa_sin]) * (scale / period),
            jnp.stack([-fa_sin, fa_cos]) * (1.0 / period),
        ]
    )
    middle = contract("npcd,pqdb->nqcb", spectrum, back_table)
    middle_re = middle[:, 0]
    middle_im = middle[:, 1]
    turned = jnp.stack(
        [middle_re * tw_cos + middle_im * tw_sin, middle_im * tw_cos - middle_re * tw_sin], 1
    )
    result = contract("rqac,nqcb->nrab", last_table, turned)
    length = half * factor_b
    return (result[:, 0].reshape(channels, length), result[:, 1].reshape(channels, length))


def depthwise(extended, kernel):
    result = lax.conv_general_dilated(
        extended[None],
        kernel[:, None, :],
        (1,),
        "VALID",
        dimension_numbers=("NWC", "WIO", "NWC"),
        feature_group_count=extended.shape[1],
        preferred_element_type=jnp.float32,
    )
    return result[0]


def per_device(
    incoming, layer_input, pre_gate, mid_gate, long_gate, out_gate, long_filter, mid_filter
):
    sections = lax.axis_size("section")
    beta = (2.0 * sections) ** (-0.5)
    adjoint = passed_along(incoming[0], "section", -1).astype(jnp.float32)
    inputs = layer_input[0].astype(jnp.float32)
    tokens = inputs.shape[0]
    gate_pre = pre_gate[0].astype(jnp.float32)
    gate_mid = mid_gate[0].astype(jnp.float32)
    gate_long = long_gate[0].astype(jnp.float32)
    gate_out = out_gate[0].astype(jnp.float32)
    filter_taps = mid_filter[0]
    reach = filter_taps.shape[0] - 1
    seq_len = tokens * lax.axis_size("ctx")
    scale = float(seq_len) ** (-0.5)
    mixed_in = (inputs * gate_pre).astype(jnp.bfloat16)
    earlier = shifted(mixed_in[tokens - reach :], "ctx", 1)
    extended = jnp.concatenate([earlier, mixed_in], 0)
    branch = depthwise(extended, filter_taps[::-1])
    resid = inputs + beta * branch * gate_mid
    long_in = (resid * gate_long).astype(jnp.bfloat16)
    grad_z = (beta * adjoint * gate_out).astype(jnp.bfloat16)
    channel_z, channel_w = (
        lax.all_to_all(grad_z.T, "ctx", split_axis=0, concat_axis=1, tiled=True),
        lax.all_to_all(long_in.T, "ctx", split_axis=0, concat_axis=1, tiled=True),
    )
    factor_b = math.gcd(seq_len, 128)
    factor_a = 2 * seq_len // factor_b
    zspec = to_spectrum(channel_z[:, None], factor_a, factor_b)
    zspec_re = zspec[:, 0]
    zspec_im = zspec[:, 1]
    pair = to_spectrum(jnp.stack([channel_w, -long_filter[0]], 1), factor_a, factor_b)
    pair_re = pair[:, 0]
    pair_im = pair[:, 1]
    joint_re = zspec_re * pair_re + zspec_im * pair_im
    joint_im = zspec_im * pair_re - zspec_re * pair_im
    lag_grad, input_part = from_spectrum(
        jnp.stack([joint_re, joint_im], 1), factor_a, factor_b, scale
    )
    long_grad = lag_grad.astype(jnp.bfloat16)[None]
    returned = lax.all_to_all(
        input_part.astype(jnp.bfloat16), "ctx", split_axis=1, concat_axis=0, tiled=True
    ).T
    grad_u = adjoint + returned.astype(jnp.float32) * gate_long
    grad_b = (beta * grad_u * gate_mid).astype(jnp.bfloat16)
    later = shifted(grad_b[:reach], "ctx", -1)
    grad_act = depthwise(jnp.concatenate([grad_b, later], 0), filter_taps)
    input_grad = (grad_u + grad_act * gate_pre).astype(jnp.bfloat16)[None]
    tap_part = depthwise(extended, grad_b)[::-1]
    total_taps = lax.psum(tap_part, "ctx")
    columns = tap_part.shape[1] // lax.axis_size("ctx")
    own_taps = lax.dynamic_slice_in_dim(total_taps, lax.axis_index("ctx") * columns, columns, 1)
    mid_grad = (own_taps * scale).astype(jnp.bfloat16)[None]
    return (input_grad, long_grad, mid_grad)


def solution(mesh):
    placed = (
        P("section", "ctx", None),
        P("section", "ctx", None),
        P("section", "ctx", None),
        P("section", "ctx", None),
        P("section", "ctx", None),
        P("section", "ctx", None),
        P("section", "ctx", None),
        P("section", None, None),
    )
    return jax.shard_map(
        per_device,
        mesh=mesh,
        in_specs=placed,
        out_specs=(P("section", "ctx", None), P("section", "ctx", None), P("section", None, "ctx")),
        check_vma=False,
    )
```

profile of v0, /device:TPU:8, one launch (start us, length us, event | category | flops | bytes accessed | tf_op | source)
XLA Modules:
  0.0 467.0 jit_solution(479754405011131320)
XLA Ops:
  10.3 2.7 collective-permute-start.1
  16.3 27.4 %convolution_multiply_fusion = f32[1,128,4096]{2,0,1:T(1,128)S(1)} fusion(bf16[1,255,4096]{2,1,0:T(8,128)(2,1)S(1)} %maximum_bitcast_fusion.13, bf16[128,1,4096]{2,0,1:T(8,128)(2,1)S(1)} %bitcast.188), kind=kOutput, calls=%fused_computation.15 | convolution fusion | flops 134742016 | bytes 5234688 | tf_op jit(solution)/shard_map/conv_general_dilated | solution.py:81
  43.7 2.1 fusion.34
  47.1 24.9 %all-to-all-start.1 = ((bf16[64,64,128]{2,1,0:T(8,128)(2,1)}), bf16[64,64,128]{2,1,0:T(8,128)(2,1)S(1)}, u32[]{:S(2)}, u32[]{:S(2)}) async-start(bf16[64,64,128]{2,1,0:T(8,128)(2,1)} %bitcast.35), calls=%async_computation.1 | async-start | bytes 2097152 | tf_op jit(solution)/shard_map/all_to_all | solution.py:118
  72.5 24.9 %collective-permute-done = bf16[128,4096]{1,0:T(8,128)(2,1)S(1)} collective-permute-done((bf16[128,4096]{1,0:T(8,128)(2,1)}, bf16[128,4096]{1,0:T(8,128)(2,1)S(1)}, u32[]{:S(2)}, u32[]{:S(2)}) %collective-permute-start) | collective-permute-done | bytes 1048608 | tf_op jit(solution)/shard_map/ppermute | solution.py:11
  100.9 10.9 %all-to-all-start = ((bf16[64,64,128]{2,1,0:T(8,128)(2,1)}), bf16[64,64,128]{2,1,0:T(8,128)(2,1)}, u32[]{:S(2)}, u32[]{:S(2)}) async-start(bf16[64,64,128]{2,1,0:T(8,128)(2,1)} %bitcast.183), calls=%async_computation | async-start | bytes 2097152 | tf_op jit(solution)/shard_map/all_to_all | solution.py:117
  117.0 5.7 %convolution_bitcast_fusion.1 = f32[64,2,128,128]{2,3,1,0:T(8,128)} fusion(bf16[64,1,64,128]{3,2,1,0:T(8,128)(2,1)S(1)} %bitcast.184, bf16[64,1,64,128]{3,2,1,0:T(8,128)(2,1)S(1)} %bitcast.185, f32[1,2,128,64]{2,3,0,1:T(8,128)S(1)} %get-tuple-element.33, f32[1,2,128,64]{2,3,0,1:T(8,128)S(1)} %get-tuple-element.32), kind=kOutput, calls=%fused_computation.34 | convolution fusion | flops 1614839808 | bytes 10616832 | tf_op jit(solution)/shard_map/qrca,nrab->nqcb/dot_general | solution.py:28
  122.7 17.8 %all-to-all-done = bf16[64,64,128]{2,1,0:T(8,128)(2,1)} async-done(((bf16[64,64,128]{2,1,0:T(8,128)(2,1)}), bf16[64,64,128]{2,1,0:T(8,128)(2,1)}, u32[]{:S(2)}, u32[]{:S(2)}) %all-to-all-start) | async-done | bytes 1048608 | tf_op jit(solution)/shard_map/all_to_all | solution.py:117
  140.5 3.8 convolution_bitcast_fusion
  144.3 5.8 %multiply_subtract_fusion.3 = (f32[64,1,128,128]{2,3,1,0:T(8,128)}, f32[64,1,128,128]{2,3,1,0:T(8,128)}, f32[64,1,128,128]{2,3,1,0:T(8,128)S(1)}, f32[64,1,128,128]{2,3,1,0:T(8,128)}) fusion(f32[64,2,128,128]{2,3,1,0:T(8,128)S(1)} %convolution_bitcast_fusion, f32[128,128]{0,1:T(8,128)S(1)} %get-tuple-element.36, f32[128,128]{0,1:T(8,128)S(1)} %get-tuple-element.37, ...), kind=kLoop, calls=%fused_computation.24 | loop fusion | flops 12582912 | bytes 33685504 | tf_op jit(solution)/shard_map/sub | solution.py:50
  150.1 7.0 %fusion.20 = f32[64,2,128,128]{2,3,0,1:T(8,128)S(1)} fusion(f32[64,1,128,128]{2,3,1,0:T(8,128)} %get-tuple-element.17, f32[64,1,128,128]{2,3,1,0:T(8,128)} %get-tuple-element.16, f32[1,2,128,128]{2,3,0,1:T(8,128)S(1)} %get-tuple-element.23, f32[1,2,128,128]{2,3,0,1:T(8,128)S(1)} %get-tuple-element.28), kind=kOutput, calls=%fused_computation.33 | convolution fusion | flops 3223388160 | bytes 17039360 | tf_op jit(solution)/shard_map/nqcb,qpbd->npcd/dot_general | solution.py:28
  157.1 4.9 %fusion.19 = f32[64,2,128,128]{2,3,0,1:T(8,128)S(1)} fusion(f32[64,1,128,128]{2,3,1,0:T(8,128)S(1)} %get-tuple-element.26, f32[64,1,128,128]{2,3,1,0:T(8,128)S(1)} %copy-done.3, f32[1,2,128,128]{2,3,0,1:T(8,128)S(1)} %get-tuple-element.23, f32[1,2,128,128]{2,3,0,1:T(8,128)S(1)} %get-tuple-element.28), kind=kOutput, calls=%fused_computation.32 | convolution fusion | flops 3223388160 | bytes 17039360 | tf_op jit(solution)/shard_map/nqcb,qpbd->npcd/dot_general | solution.py:28
  163.9 5.0 %fusion.16 = f32[64,2,128,128]{2,3,1,0:T(8,128)S(1)} fusion(f32[64,1,128,128]{2,3,0,1:T(8,128)S(1)} %get-tuple-element.13, f32[64,1,128,128]{2,3,0,1:T(8,128)S(1)} %get-tuple-element.12, f32[1,2,128,128]{2,3,1,0:T(8,128)S(1)} %copy-done.20, f32[1,2,128,128]{2,3,1,0:T(8,128)S(1)} %copy-done.19), kind=kOutput, calls=%fused_computation.30 | convolution fusion | flops 3223388160 | bytes 17039360 | tf_op jit(solution)/shard_map/npcd,pqdb->nqcb/dot_general | solution.py:28
  170.9 4.6 fusion.33
  177.3 5.6 %all-to-all-start.2 = ((bf16[64,64,128]{2,0,1:T(8,128)(2,1)}), bf16[64,64,128]{2,0,1:T(8,128)(2,1)S(1)}, u32[]{:S(2)}, u32[]{:S(2)}) async-start(bf16[64,64,128]{2,0,1:T(8,128)(2,1)} %copy.65), calls=%async_computation.2 | async-start | bytes 2097152 | tf_op jit(solution)/shard_map/all_to_all | solution.py:134
  184.2 27.6 %all-to-all-done.2 = bf16[64,64,128]{2,0,1:T(8,128)(2,1)S(1)} async-done(((bf16[64,64,128]{2,0,1:T(8,128)(2,1)}), bf16[64,64,128]{2,0,1:T(8,128)(2,1)S(1)}, u32[]{:S(2)}, u32[]{:S(2)}) %all-to-all-start.2) | async-done | bytes 1048608 | tf_op jit(solution)/shard_map/all_to_all | solution.py:134
  213.4 1.9 copy.66
  215.4 3.9 fusion.23
  220.5 28.8 %fusion.13 = f32[1,128,4096]{2,0,1:T(1,128)S(1)} fusion(bf16[1,255,4096]{2,1,0:T(8,128)(2,1)S(1)} %copy-done.12, bf16[128,1,4096]{2,0,1:T(8,128)(2,1)} %bitcast.72), kind=kOutput, calls=%fused_computation.27 | convolution fusion | flops 134217728 | bytes 5234688 | tf_op jit(solution)/shard_map/conv_general_dilated | solution.py:81
  249.3 3.0 copy.131
  252.3 16.6 %rev.7 = f32[128,4096]{1,0:T(8,128)} reverse(f32[128,4096]{1,0:T(8,128)} %bitcast.182), dimensions={0} | reverse | bytes 4194304 | tf_op jit(solution)/shard_map/rev | solution.py:142
  270.6 30.1 %fusion.11 = f32[1,128,4096]{2,0,1:T(1,128)S(1)} fusion(bf16[1,255,4096]{2,1,0:T(8,128)(2,1)S(1)} %maximum_bitcast_fusion.16, bf16[128,1,4096]{2,0,1:T(8,128)(2,1)S(1)} %bitcast.187), kind=kOutput, calls=%fused_computation.25 | convolution fusion | flops 134217728 | bytes 5234688 | tf_op jit(solution)/shard_map/conv_general_dilated | solution.py:81
  300.7 2.8 fusion.35
  303.6 154.7 %all-reduce.2.cloned.1.call-done = f32[128,4096]{1,0:T(8,128)} async-done(((f32[128,4096]{1,0:T(8,128)}), f32[128,4096]{1,0:T(8,128)}) %all-reduce.2.cloned.1.call-update) | async-done | bytes 2097168 | tf_op jit(solution)/shard_map/psum | solution.py:143
  (78 shorter events, 29.7 us)
Async XLA Ops:
  7.2 5.9 %copy-start.13 = (bf16[1,128,4096]{2,1,0:T(8,128)(2,1)S(1)}, bf16[1,128,4096]{2,1,0:T(8,128)(2,1)}, u32[]{:S(2)}) copy-start(bf16[1,128,4096]{2,1,0:T(8,128)(2,1)} %param.15) | copy-start | bytes 3145732
  10.3 4.3 collective-permute-start.1
  16.2 27.5 %copy-start.11 = (bf16[1,255,4096]{2,1,0:T(8,128)(2,1)}, bf16[1,255,4096]{2,1,0:T(8,128)(2,1)S(1)}, u32[]{:S(2)}) copy-start(bf16[1,255,4096]{2,1,0:T(8,128)(2,1)S(1)} %maximum_bitcast_fusion.13) | copy-start | bytes 6266884
  16.2 27.5 %copy-start.6 = (bf16[1,128,4096]{2,1,0:T(8,128)(2,1)S(1)}, bf16[1,128,4096]{2,1,0:T(8,128)(2,1)}, u32[]{:S(2)}) copy-start(bf16[1,128,4096]{2,1,0:T(8,128)(2,1)} %param.12) | copy-start | bytes 3145732
  16.2 27.5 %copy-start.8 = (bf16[1,128,4096]{2,1,0:T(8,128)(2,1)S(1)}, bf16[1,128,4096]{2,1,0:T(8,128)(2,1)}, u32[]{:S(2)}) copy-start(bf16[1,128,4096]{2,1,0:T(8,128)(2,1)} %param.9) | copy-start | bytes 3145732
  16.2 27.5 %copy-start.9 = (bf16[1,128,4096]{2,1,0:T(8,128)(2,1)S(1)}, bf16[1,128,4096]{2,1,0:T(8,128)(2,1)}, u32[]{:S(2)}) copy-start(bf16[1,128,4096]{2,1,0:T(8,128)(2,1)} %param.11) | copy-start | bytes 3145732
  47.1 53.8 %all-to-all-start.1 = ((bf16[64,64,128]{2,1,0:T(8,128)(2,1)}), bf16[64,64,128]{2,1,0:T(8,128)(2,1)S(1)}, u32[]{:S(2)}, u32[]{:S(2)}) async-start(bf16[64,64,128]{2,1,0:T(8,128)(2,1)} %bitcast.35), calls=%async_computation.1 | async-start | bytes 2097152 | tf_op jit(solution)/shard_map/all_to_all | solution.py:118
  72.0 25.4 %collective-permute-start = (bf16[128,4096]{1,0:T(8,128)(2,1)}, bf16[128,4096]{1,0:T(8,128)(2,1)S(1)}, u32[]{:S(2)}, u32[]{:S(2)}) collective-permute-start(bf16[128,4096]{1,0:T(8,128)(2,1)} %bitcast.189), channel_id=1, source_target_pairs={{0,192},{64,0},{128,64},{192,128},{1,193},{65,1},{129,65},{193,129... | collective-permute-start | bytes 3145736 | tf_op jit(solution)/shard_map/ppermute | solution.py:11
  97.4 117.9 %copy-start.4 = (bf16[128,4096]{1,0:T(8,128)(2,1)}, bf16[128,4096]{1,0:T(8,128)(2,1)S(1)}, u32[]{:S(2)}) copy-start(bf16[128,4096]{1,0:T(8,128)(2,1)S(1)} %collective-permute-done) | copy-start | bytes 3145732
  100.9 39.6 %all-to-all-start = ((bf16[64,64,128]{2,1,0:T(8,128)(2,1)}), bf16[64,64,128]{2,1,0:T(8,128)(2,1)}, u32[]{:S(2)}, u32[]{:S(2)}) async-start(bf16[64,64,128]{2,1,0:T(8,128)(2,1)} %bitcast.183), calls=%async_computation | async-start | bytes 2097152 | tf_op jit(solution)/shard_map/all_to_all | solution.py:117
  114.9 2.1 copy-start.15
  114.9 2.1 copy-start.16
  140.5 3.8 copy-start
  150.1 7.0 %copy-start.3 = (f32[64,1,128,128]{2,3,1,0:T(8,128)S(1)}, f32[64,1,128,128]{2,3,1,0:T(8,128)}, u32[]{:S(2)}) copy-start(f32[64,1,128,128]{2,3,1,0:T(8,128)} %get-tuple-element.27) | copy-start | bytes 12582916
  168.9 1.9 copy-start.17
  177.3 34.5 %all-to-all-start.2 = ((bf16[64,64,128]{2,0,1:T(8,128)(2,1)}), bf16[64,64,128]{2,0,1:T(8,128)(2,1)S(1)}, u32[]{:S(2)}, u32[]{:S(2)}) async-start(bf16[64,64,128]{2,0,1:T(8,128)(2,1)} %copy.65), calls=%async_computation.2 | async-start | bytes 2097152 | tf_op jit(solution)/shard_map/all_to_all | solution.py:134
  182.9 275.3 %all-reduce.2.cloned.1.call-start = ((), (), s32[]{:S(2)}) async-start(), calls=%async_computation.3 | async-start | bytes 4194304 | tf_op jit(solution)/shard_map/psum | solution.py:143
  215.3 34.0 %copy-start.1 = (f32[4096,128]{0,1:T(8,128)}, f32[4096,128]{0,1:T(8,128)S(1)}, u32[]{:S(2)}) copy-start(f32[4096,128]{0,1:T(8,128)S(1)} %copy.66) | copy-start | bytes 6291460
  215.3 5.2 %copy-start.12 = (bf16[1,255,4096]{2,1,0:T(8,128)(2,1)S(1)}, bf16[1,255,4096]{2,1,0:T(8,128)(2,1)}, u32[]{:S(2)}) copy-start(bf16[1,255,4096]{2,1,0:T(8,128)(2,1)} %copy-done.11) | copy-start | bytes 6266884
  219.2 49.7 %collective-permute-start.2 = (bf16[127,4096]{1,0:T(8,128)(2,1)}, bf16[127,4096]{1,0:T(8,128)(2,1)S(1)}, u32[]{:S(2)}, u32[]{:S(2)}) collective-permute-start(bf16[127,4096]{1,0:T(8,128)(2,1)} %bitcast.180), channel_id=1, source_target_pairs={{1,0},{2,1},{3,2},{4,3},{5,4},{6,5},{7,6},{8,7},{9,8},{10,9},{11,1... | collective-permute-start | bytes 3121160 | tf_op jit(solution)/shard_map/ppermute | solution.py:17
  270.5 30.2 %copy-start.2 = (f32[4096,128]{0,1:T(8,128)S(1)}, f32[4096,128]{0,1:T(8,128)}, u32[]{:S(2)}) copy-start(f32[4096,128]{0,1:T(8,128)} %copy-done.1) | copy-start | bytes 6291460
  270.5 30.2 %copy-start.5 = (bf16[128,4096]{1,0:T(8,128)(2,1)S(1)}, bf16[128,4096]{1,0:T(8,128)(2,1)}, u32[]{:S(2)}) copy-start(bf16[128,4096]{1,0:T(8,128)(2,1)} %copy-done.4) | copy-start | bytes 3145732
  270.6 30.2 %copy-start.7 = (bf16[1,128,4096]{2,1,0:T(8,128)(2,1)S(1)}, bf16[1,128,4096]{2,1,0:T(8,128)(2,1)}, u32[]{:S(2)}) copy-start(bf16[1,128,4096]{2,1,0:T(8,128)(2,1)} %param.12) | copy-start | bytes 3145732
  270.6 30.2 %copy-start.10 = (bf16[1,128,4096]{2,1,0:T(8,128)(2,1)S(1)}, bf16[1,128,4096]{2,1,0:T(8,128)(2,1)}, u32[]{:S(2)}) copy-start(bf16[1,128,4096]{2,1,0:T(8,128)(2,1)} %param.10) | copy-start | bytes 3145732
  (4 other events, 7.2 us)
Sparse Core Ops, SparseCore 0:
  269.1 189.1 all-reduce.1
where the time goes:
time: 474 us; the launch traced here: 467 us
  waiting for transfers between devices  226 us (48%)
  matrix products  117 us (25%)
  starting transfers between devices  45.9 us (10%)
  other arithmetic  31.9 us (7%)
  local copies, waits for them, and re-layouts  31.5 us (7%)
  between operations  14.8 us (3%)
    psum x1, waiting for transfers between devices, per_device(): total_taps = lax.psum(tap_part, 'ctx')  155 us
    conv_general_dilated x3, matrix products, depthwise(): lax.conv_general_dilated(extended[None], kernel[:, None, :], (1,), 'VALID...  86.3 us
    dot_general x6, matrix products, contract(): jnp.einsum(form, left, right, precision=lax.Precision.HIGH, preferred_ele...  31 us
    all_to_all x1, waiting for transfers between devices, per_device(): lax.all_to_all(input_part.astype(jnp.bfloat16), 'ctx', split_axis=1, conc...  27.6 us
    ppermute x1, waiting for transfers between devices, passed_along(): return lax.ppermute(value, axis, pairs)  24.9 us
    all_to_all x1, starting transfers between devices, per_device(): lax.all_to_all(long_in.T, 'ctx', split_axis=0, concat_axis=1, tiled=True)  24.9 us
    all_to_all x1, waiting for transfers between devices, per_device(): lax.all_to_all(grad_z.T, 'ctx', split_axis=0, concat_axis=1, tiled=True)  17.8 us
    rev x1, local copies, waits for them, and re-layouts, per_device(): tap_part = depthwise(extended, grad_b)[::-1]  16.6 us
  transfers between devices with their start and end apart: 7, of which 6 were waited for; matrix products, arithmetic and copies ran while one was open for 21% of the time, Pallas kernels for 0%

commit v1 on v0

--- a/solution.py
+++ b/solution.py
@@ -140,7 +140,7 @@
     grad_act = depthwise(jnp.concatenate([grad_b, later], 0), filter_taps)
     input_grad = (grad_u + grad_act * gate_pre).astype(jnp.bfloat16)[None]
     tap_part = depthwise(extended, grad_b)[::-1]
-    total_taps = lax.psum(tap_part, "ctx")
+    total_taps = jnp.sum(lax.all_gather(tap_part, "ctx"), axis=0)
     columns = tap_part.shape[1] // lax.axis_size("ctx")
     own_taps = lax.dynamic_slice_in_dim(total_taps, lax.axis_index("ctx") * columns, columns, 1)
     mid_grad = (own_taps * scale).astype(jnp.bfloat16)[None]

time: 474 us -> 760 us (1.60)
  waiting for transfers between devices: 226 us -> 440 us
  other arithmetic: 31.9 us -> 71.2 us
  blocking collectives: 0 us -> 34.4 us
    all_gather x0 -> x1, waiting for transfers between devices: none -> 395 us  [per_device(): total_taps = jnp.sum(lax.all_gather(tap_part, 'ctx'), axis=0)]
    psum x1 -> x0, waiting for transfers between devices: 155 us -> none  [per_device(): total_taps = lax.psum(tap_part, 'ctx')]
    reduce_sum x0 -> x1, other arithmetic: none -> 40.6 us  [per_device(): total_taps = jnp.sum(lax.all_gather(tap_part, 'ctx'), axis=0)]
    all_to_all x0 -> x1, blocking collectives: none -> 34.4 us  [per_device(): lax.all_to_all(input_part.astype(jnp.bfloat16), 'ctx', split_axis=1, conc...]
    all_to_all x1 -> x0, waiting for transfers between devices: 27.6 us -> none  [per_device(): lax.all_to_all(input_part.astype(jnp.bfloat16), 'ctx', split_axis=1, conc...]
  transfers between devices with their start and end apart: 7 -> 6, of which waited for: 6 -> 6; matrix products, arithmetic and copies ran while one was open for 21% -> 7% of each run, Pallas kernels for 0% -> 0%
where the time goes in v1:
time: 760 us; the launch traced here: 751 us
  waiting for transfers between devices  440 us (58%)
  matrix products  118 us (16%)
  other arithmetic  71.2 us (9%)
  starting transfers between devices  40.3 us (5%)
  blocking collectives  34.4 us (5%)
  local copies, waits for them, and re-layouts  31.6 us (4%)
  between operations  14.8 us (2%)
    all_gather x1, waiting for transfers between devices, per_device(): total_taps = jnp.sum(lax.all_gather(tap_part, 'ctx'), axis=0)  395 us
    conv_general_dilated x3, matrix products, depthwise(): lax.conv_general_dilated(extended[None], kernel[:, None, :], (1,), 'VALID...  87.6 us
    reduce_sum x1, other arithmetic, per_device(): total_taps = jnp.sum(lax.all_gather(tap_part, 'ctx'), axis=0)  40.6 us
    all_to_all x1, blocking collectives, per_device(): lax.all_to_all(input_part.astype(jnp.bfloat16), 'ctx', split_axis=1, conc...  34.4 us
    dot_general x6, matrix products, contract(): jnp.einsum(form, left, right, precision=lax.Precision.HIGH, preferred_ele...  30.6 us
    ppermute x1, waiting for transfers between devices, passed_along(): return lax.ppermute(value, axis, pairs)  24.9 us
    all_to_all x1, starting transfers between devices, per_device(): lax.all_to_all(long_in.T, 'ctx', split_axis=0, concat_axis=1, tiled=True)  24.9 us
    all_to_all x1, waiting for transfers between devices, per_device(): lax.all_to_all(grad_z.T, 'ctx', split_axis=0, concat_axis=1, tiled=True)  17.5 us
  transfers between devices with their start and end apart: 6, of which 6 were waited for; matrix products, arithmetic and copies ran while one was open for 7% of the time, Pallas kernels for 0%

profile of v1, /device:TPU:8, one launch (start us, length us, event | category | flops | bytes accessed | tf_op | source)
XLA Modules:
  0.0 750.9 jit_solution(6489696355337215958)
XLA Ops:
  10.3 2.7 collective-permute-start.1
  16.2 27.4 %convolution_multiply_fusion = f32[1,128,4096]{2,0,1:T(1,128)S(1)} fusion(bf16[1,255,4096]{2,1,0:T(8,128)(2,1)S(1)} %maximum_bitcast_fusion.13, bf16[128,1,4096]{2,0,1:T(8,128)(2,1)S(1)} %bitcast.191), kind=kOutput, calls=%fused_computation.15 | convolution fusion | flops 134742016 | bytes 5234688 | tf_op jit(solution)/shard_map/conv_general_dilated | solution.py:81
  43.7 2.1 fusion.34
  47.1 24.9 %all-to-all-start.1 = ((bf16[64,64,128]{2,1,0:T(8,128)(2,1)}), bf16[64,64,128]{2,1,0:T(8,128)(2,1)S(1)}, u32[]{:S(2)}, u32[]{:S(2)}) async-start(bf16[64,64,128]{2,1,0:T(8,128)(2,1)} %bitcast.35), calls=%async_computation.1 | async-start | bytes 2097152 | tf_op jit(solution)/shard_map/all_to_all | solution.py:118
  72.5 24.9 %collective-permute-done = bf16[128,4096]{1,0:T(8,128)(2,1)S(1)} collective-permute-done((bf16[128,4096]{1,0:T(8,128)(2,1)}, bf16[128,4096]{1,0:T(8,128)(2,1)S(1)}, u32[]{:S(2)}, u32[]{:S(2)}) %collective-permute-start) | collective-permute-done | bytes 1048608 | tf_op jit(solution)/shard_map/ppermute | solution.py:11
  100.8 10.4 %all-to-all-start = ((bf16[64,64,128]{2,1,0:T(8,128)(2,1)}), bf16[64,64,128]{2,1,0:T(8,128)(2,1)}, u32[]{:S(2)}, u32[]{:S(2)}) async-start(bf16[64,64,128]{2,1,0:T(8,128)(2,1)} %bitcast.184), calls=%async_computation | async-start | bytes 2097152 | tf_op jit(solution)/shard_map/all_to_all | solution.py:117
  116.8 5.7 convolution_bitcast_fusion.1
  122.5 17.5 %all-to-all-done = bf16[64,64,128]{2,1,0:T(8,128)(2,1)} async-done(((bf16[64,64,128]{2,1,0:T(8,128)(2,1)}), bf16[64,64,128]{2,1,0:T(8,128)(2,1)}, u32[]{:S(2)}, u32[]{:S(2)}) %all-to-all-start) | async-done | bytes 1048608 | tf_op jit(solution)/shard_map/all_to_all | solution.py:117
  140.0 3.8 convolution_bitcast_fusion
  143.8 6.4 multiply_subtract_fusion.3
  150.2 6.8 fusion.19
  157.0 4.9 fusion.20
  163.9 5.0 fusion.16
  170.9 4.4 fusion.33
  177.2 34.4 %all_to_all.42 = bf16[64,64,128]{2,0,1:T(8,128)(2,1)S(1)} all-to-all(bf16[64,64,128]{2,0,1:T(8,128)(2,1)S(1)} %copy.63), channel_id=1, replica_groups=mesh['section'=4,'ctx'=64] {'ctx'}, dimensions={1} | all-to-all | bytes 2097152 | tf_op jit(solution)/shard_map/all_to_all | solution.py:134
  215.2 2.9 fusion.23
  218.1 30.1 %fusion.13 = f32[1,128,4096]{2,0,1:T(1,128)S(1)} fusion(bf16[1,255,4096]{2,1,0:T(8,128)(2,1)S(1)} %copy-done.15, bf16[128,1,4096]{2,0,1:T(8,128)(2,1)S(1)} %bitcast.185), kind=kOutput, calls=%fused_computation.27 | convolution fusion | flops 134217728 | bytes 5234688 | tf_op jit(solution)/shard_map/conv_general_dilated | solution.py:81
  248.3 3.0 copy.129
  251.3 16.8 %rev.7 = f32[128,4096]{1,0:T(8,128)} reverse(f32[128,4096]{1,0:T(8,128)} %bitcast.183), dimensions={0} | reverse | bytes 4194304 | tf_op jit(solution)/shard_map/rev | solution.py:142
  270.8 2.1 collective-permute-done.2
  274.4 30.1 %fusion.11 = f32[1,128,4096]{2,0,1:T(1,128)S(1)} fusion(bf16[1,255,4096]{2,1,0:T(8,128)(2,1)S(1)} %maximum_bitcast_fusion.16, bf16[128,1,4096]{2,0,1:T(8,128)(2,1)S(1)} %bitcast.190), kind=kOutput, calls=%fused_computation.25 | convolution fusion | flops 134217728 | bytes 5234688 | tf_op jit(solution)/shard_map/conv_general_dilated | solution.py:81
  304.5 2.8 fusion.35
  307.3 395.1 %all-gather.3.cloned.1.call-done = f32[8192,4096]{1,0:T(8,128)} async-done(((f32[128,4096]{1,0:T(8,128)}), f32[8192,4096]{1,0:T(8,128)}) %all-gather.3.cloned.1.call-update) | async-done | bytes 134217744 | tf_op jit(solution)/shard_map/all_gather | solution.py:143
  702.4 40.6 %reduce_sum.9 = f32[128,4096]{1,0:T(8,128)S(1)} reduce(f32[64,128,4096]{2,1,0:T(8,128)} %bitcast.73, f32[]{:T(128)} %constant.83.clone.1), dimensions={0}, to_apply=%region_0.1 | reduce | flops 33030144 | bytes 136314880 | tf_op jit(solution)/shard_map/reduce_sum | solution.py:143
  (84 shorter events, 31.3 us)
Async XLA Ops:
  7.2 5.9 copy-start.16
  10.3 4.3 collective-permute-start.1
  16.2 27.5 %copy-start.14 = (bf16[1,255,4096]{2,1,0:T(8,128)(2,1)}, bf16[1,255,4096]{2,1,0:T(8,128)(2,1)S(1)}, u32[]{:S(2)}) copy-start(bf16[1,255,4096]{2,1,0:T(8,128)(2,1)S(1)} %maximum_bitcast_fusion.13) | copy-start | bytes 6266884
  16.2 27.5 %copy-start.6 = (bf16[1,128,4096]{2,1,0:T(8,128)(2,1)S(1)}, bf16[1,128,4096]{2,1,0:T(8,128)(2,1)}, u32[]{:S(2)}) copy-start(bf16[1,128,4096]{2,1,0:T(8,128)(2,1)} %param.12) | copy-start | bytes 3145732
  16.2 27.5 %copy-start.8 = (bf16[1,128,4096]{2,1,0:T(8,128)(2,1)S(1)}, bf16[1,128,4096]{2,1,0:T(8,128)(2,1)}, u32[]{:S(2)}) copy-start(bf16[1,128,4096]{2,1,0:T(8,128)(2,1)} %param.9) | copy-start | bytes 3145732
  16.2 27.5 %copy-start.10 = (bf16[1,128,4096]{2,1,0:T(8,128)(2,1)S(1)}, bf16[1,128,4096]{2,1,0:T(8,128)(2,1)}, u32[]{:S(2)}) copy-start(bf16[1,128,4096]{2,1,0:T(8,128)(2,1)} %param.11) | copy-start | bytes 3145732
  47.1 53.8 %all-to-all-start.1 = ((bf16[64,64,128]{2,1,0:T(8,128)(2,1)}), bf16[64,64,128]{2,1,0:T(8,128)(2,1)S(1)}, u32[]{:S(2)}, u32[]{:S(2)}) async-start(bf16[64,64,128]{2,1,0:T(8,128)(2,1)} %bitcast.35), calls=%async_computation.1 | async-start | bytes 2097152 | tf_op jit(solution)/shard_map/all_to_all | solution.py:118
  71.9 25.4 %collective-permute-start = (bf16[128,4096]{1,0:T(8,128)(2,1)}, bf16[128,4096]{1,0:T(8,128)(2,1)S(1)}, u32[]{:S(2)}, u32[]{:S(2)}) collective-permute-start(bf16[128,4096]{1,0:T(8,128)(2,1)} %bitcast.192), channel_id=1, source_target_pairs={{0,192},{64,0},{128,64},{192,128},{1,193},{65,1},{129,65},{193,129... | collective-permute-start | bytes 3145736 | tf_op jit(solution)/shard_map/ppermute | solution.py:11
  97.4 117.8 %copy-start.4 = (bf16[128,4096]{1,0:T(8,128)(2,1)}, bf16[128,4096]{1,0:T(8,128)(2,1)S(1)}, u32[]{:S(2)}) copy-start(bf16[128,4096]{1,0:T(8,128)(2,1)S(1)} %collective-permute-done) | copy-start | bytes 3145732
  100.8 39.1 %all-to-all-start = ((bf16[64,64,128]{2,1,0:T(8,128)(2,1)}), bf16[64,64,128]{2,1,0:T(8,128)(2,1)}, u32[]{:S(2)}, u32[]{:S(2)}) async-start(bf16[64,64,128]{2,1,0:T(8,128)(2,1)} %bitcast.184), calls=%async_computation | async-start | bytes 2097152 | tf_op jit(solution)/shard_map/all_to_all | solution.py:117
  111.2 591.2 %all-gather.3.cloned.1.call-start = ((), (), s32[]{:S(2)}) async-start(), calls=%async_computation.3 | async-start | bytes 136314880 | tf_op jit(solution)/shard_map/all_gather | solution.py:143
  140.0 3.8 copy-start
  150.2 6.8 copy-start.3
  215.1 33.1 %copy-start.1 = (f32[4096,128]{0,1:T(8,128)}, f32[4096,128]{0,1:T(8,128)S(1)}, u32[]{:S(2)}) copy-start(f32[4096,128]{0,1:T(8,128)S(1)} %copy.64) | copy-start | bytes 6291460
  215.2 3.0 copy-start.15
  218.1 30.2 %copy-start.12 = (bf16[128,4096]{1,0:T(8,128)(2,1)}, bf16[128,4096]{1,0:T(8,128)(2,1)S(1)}, u32[]{:S(2)}) copy-start(bf16[128,4096]{1,0:T(8,128)(2,1)S(1)} %fusion.23) | copy-start | bytes 3145732
  251.3 16.8 %copy-start.13 = (bf16[128,4096]{1,0:T(8,128)(2,1)S(1)}, bf16[128,4096]{1,0:T(8,128)(2,1)}, u32[]{:S(2)}) copy-start(bf16[128,4096]{1,0:T(8,128)(2,1)} %copy-done.12) | copy-start | bytes 3145732
  251.3 18.2 %copy-start.9 = (bf16[64,1,64,128]{3,2,1,0:T(8,128)(2,1)S(1)}, bf16[64,1,64,128]{3,2,1,0:T(8,128)(2,1)}, u32[]{:S(2)}) copy-start(bf16[64,1,64,128]{3,2,1,0:T(8,128)(2,1)} %get-tuple-element.14) | copy-start | bytes 3145732
  268.0 6.3 copy-start.17
  268.1 4.8 collective-permute-start.2
  274.3 30.2 %copy-start.2 = (f32[4096,128]{0,1:T(8,128)S(1)}, f32[4096,128]{0,1:T(8,128)}, u32[]{:S(2)}) copy-start(f32[4096,128]{0,1:T(8,128)} %copy-done.1) | copy-start | bytes 6291460
  274.3 30.2 %copy-start.5 = (bf16[128,4096]{1,0:T(8,128)(2,1)S(1)}, bf16[128,4096]{1,0:T(8,128)(2,1)}, u32[]{:S(2)}) copy-start(bf16[128,4096]{1,0:T(8,128)(2,1)} %copy-done.4) | copy-start | bytes 3145732
  274.3 30.2 %copy-start.7 = (bf16[1,128,4096]{2,1,0:T(8,128)(2,1)S(1)}, bf16[1,128,4096]{2,1,0:T(8,128)(2,1)}, u32[]{:S(2)}) copy-start(bf16[1,128,4096]{2,1,0:T(8,128)(2,1)} %param.12) | copy-start | bytes 3145732
  274.3 30.2 %copy-start.11 = (bf16[1,128,4096]{2,1,0:T(8,128)(2,1)S(1)}, bf16[1,128,4096]{2,1,0:T(8,128)(2,1)}, u32[]{:S(2)}) copy-start(bf16[1,128,4096]{2,1,0:T(8,128)(2,1)} %param.10) | copy-start | bytes 3145732
  (6 other events, 12.1 us)
Sparse Core Ops, SparseCore 0:
  268.2 434.1 all-gather.2
